TPU v7x, 32 devices: a whole 2x2x4 slice. The times are simulated.
32 devices in a mesh: row: 4 (over y, core), col: 8 (over z, x).
Axes of the slice: x: 2, y: 2, z: 4, core: 2. Of those that a mesh axis runs over, the one named last changes fastest.
Arguments:
- pair: bfloat16 [1024, 1024, 128], P('row', 'col'), may hold values from -6 to 6
- norm_gain: float32 [128], replicated, may hold values from 0.1 to 1.9
- norm_shift: float32 [128], replicated, may hold values from -3 to 3
- w_query: bfloat16 [128, 128], replicated, may hold values from -1 to 1
- w_key: bfloat16 [128, 128], replicated, may hold values from -0.5 to 0.5
- w_value: bfloat16 [128, 128], replicated, may hold values from -0.5 to 0.5
- w_gate: bfloat16 [128, 128], replicated, may hold values from -0.5 to 0.5
- gate_shift: float32 [128], replicated, may hold values from -1 to 1
- w_bias: float32 [128, 4], replicated, may hold values from -30 to 30
- w_out: bfloat16 [128, 128], replicated, may hold values from -1 to 1
- out_shift: float32 [128], replicated, may hold values from -3 to 3
Outputs:
- update: bfloat16 [1024, 1024, 128], P('row', 'col')
All inputs are finite; a program needn't handle non-finite values.
Results may differ from a plain program's by a relative error of at most 0.0015.
The roundings to bfloat16 on the way count: a program that leaves them out, or rounds other values in their place, can miss the bound.
Values may be sent and summed in bfloat16 or wider, within the bound.
A program may use at most 128 MiB of HBM per device.

v0:
```python
import math

import jax
import jax.numpy as jnp
from jax import lax
from jax.sharding import PartitionSpec as P


def normalize(values, gain, shift):
    values = values.astype(jnp.float32)
    mean = jnp.mean(values, axis=-1, keepdims=True)
    centred = values - mean
    spread = jnp.mean(centred * centred, axis=-1, keepdims=True)
    return (centred * lax.rsqrt(spread + 1e-05) * gain + shift).astype(jnp.bfloat16)


def attend_one(
    pair_row, query_rows, bias, w_query, w_key, w_value, w_gate, gate_shift, w_out, out_shift
):
    heads = bias.shape[0]
    inner = w_query.shape[1]
    depth = inner // heads
    seq_length = pair_row.shape[0]
    query_count = query_rows.shape[0]
    query = (
        jnp.dot(query_rows, w_query, preferred_element_type=jnp.float32) * (1.0 / math.sqrt(depth))
    ).astype(jnp.bfloat16)
    key = jnp.dot(pair_row, w_key, preferred_element_type=jnp.float32).astype(jnp.bfloat16)
    value = jnp.dot(pair_row, w_value, preferred_element_type=jnp.float32).astype(jnp.bfloat16)
    gate = jax.nn.sigmoid(
        jnp.dot(query_rows, w_gate, preferred_element_type=jnp.float32) + gate_shift
    )
    query = query.reshape(query_count, heads, depth)
    key = key.reshape(seq_length, heads, depth)
    value = value.reshape(seq_length, heads, depth)
    scores = jnp.einsum("jhd,khd->hjk", query, key, preferred_element_type=jnp.float32) + bias
    largest = jnp.max(scores, axis=2, keepdims=True)
    raised = jnp.exp(scores - largest)
    weights = (raised / jnp.sum(raised, axis=2, keepdims=True)).astype(jnp.bfloat16)
    attended = jnp.einsum(
        "hjk,khd->jhd", weights, value, preferred_element_type=jnp.float32
    ).reshape(query_count, inner)
    gated = (gate * attended).astype(jnp.bfloat16)
    return (jnp.dot(gated, w_out, preferred_element_type=jnp.float32) + out_shift).astype(
        jnp.bfloat16
    )


def on_device(
    pair,
    norm_gain,
    norm_shift,
    w_query,
    w_key,
    w_value,
    w_gate,
    gate_shift,
    w_bias,
    w_out,
    out_shift,
):
    params = (w_query, w_key, w_value, w_gate, gate_shift, w_out, out_shift)
    col_count = lax.axis_size("col")
    row_count = lax.axis_size("row")
    groups = 1
    while (
        groups * 2 * (groups * 2) <= col_count
        and row_count % (groups * 2) == 0
        and (col_count % (groups * 2) == 0)
    ):
        groups = groups * 2
    across = col_count // groups
    tile_rows, tile_cols, channels = pair.shape
    unit = tile_cols // row_count
    heads = w_bias.shape[1]
    tile_normed = normalize(pair, norm_gain, norm_shift)
    tile_bias = jnp.einsum(
        "jkc,ch->hjk", tile_normed.astype(jnp.float32), w_bias, precision=lax.Precision.HIGHEST
    )
    sorted_bias = tile_bias.reshape(heads, col_count // groups, groups, unit, tile_cols).transpose(
        0, 2, 1, 3, 4
    )
    send_bias = jnp.broadcast_to(
        sorted_bias[:, None], (heads, across, groups, col_count // groups, unit, tile_cols)
    )
    send_bias = send_bias.reshape(heads, col_count, col_count // groups, unit, tile_cols)
    got_bias = lax.all_to_all(send_bias, "col", split_axis=1, concat_axis=4, tiled=True)
    group_bias = lax.all_gather(got_bias, "row", axis=1, tiled=True)
    seq_length = group_bias.shape[4]
    query_bias = group_bias.reshape(heads, seq_length // groups, seq_length)
    part_rows = tile_normed.reshape(across, tile_rows // across, tile_cols, channels)
    send_rows = jnp.broadcast_to(
        part_rows[:, None], (across, groups, tile_rows // across, tile_cols, channels)
    )
    send_rows = send_rows.reshape(col_count, tile_rows // across, tile_cols, channels)
    my_rows = lax.all_to_all(send_rows, "col", split_axis=0, concat_axis=2, tiled=True)[0]
    slot = lax.axis_index("col") % groups

    def row_update(pair_row):
        split_rows = pair_row.reshape(seq_length // (groups * unit), groups, unit, channels)
        picked = lax.dynamic_slice_in_dim(split_rows, slot, 1, 1).reshape(
            seq_length // groups, channels
        )
        return attend_one(pair_row, picked, query_bias, *params)

    update_part = lax.map(row_update, my_rows)
    blocks = update_part.reshape(
        tile_rows // across, col_count, row_count // groups, unit, channels
    )
    back = lax.all_to_all(blocks, "col", split_axis=1, concat_axis=0, tiled=True)
    tile = back.reshape(across, groups, tile_rows // across, row_count // groups, unit, channels)
    return tile.transpose(0, 2, 3, 1, 4, 5).reshape(tile_rows, tile_cols, channels)


def solution(mesh):
    in_specs = (P("row", "col", None), P(), P(), P(), P(), P(), P(), P(), P(), P(), P())
    out_specs = P("row", "col", None)
    return jax.shard_map(
        on_device, mesh=mesh, in_specs=in_specs, out_specs=out_specs, check_vma=False
    )
```

profile of v0, /device:TPU:0, one launch (start us, length us, event | category | flops | bytes accessed | tf_op | source)
XLA Modules:
  0.0 1602.6 jit_solution(13077037658885256515)
XLA Ops:
  12.4 11.0 fusion.27
  23.5 10.0 fusion.30
  33.5 6.6 fusion.31
  40.4 55.3 %all_to_all.48 = f32[4,8,4,32,128]{4,3,2,0,1:T(8,128)S(1)} all-to-all(f32[4,8,4,32,128]{4,3,2,0,1:T(8,128)S(1)} %bitcast.112), channel_id=1, replica_groups=mesh['row'=4,'col'=8] {'col'}, dimensions={1} | all-to-all | bytes 4194304 | tf_op jit(solution)/shard_map/all_to_all | solution.py:87
  95.8 8.0 broadcast_in_dim.15
  113.3 59.5 %all-gather.2.cloned.1.call-done = f32[4,4,4,32,1024]{4,3,2,0,1:T(8,128)} async-done(((f32[4,1,4,32,1024]{4,3,2,0,1:T(8,128)}), f32[4,4,4,32,1024]{4,3,2,0,1:T(8,128)}) %all-gather.2.cloned.1.call-update) | async-done | bytes 8388624 | tf_op jit(solution)/shard_map/all_gather | solution.py:88
  172.8 8.3 copy.48
  181.1 290.4 %all-to-all-done = bf16[8,64,128,128]{3,2,1,0:T(8,128)(2,1)} async-done(((bf16[8,64,128,128]{3,2,1,0:T(8,128)(2,1)}), bf16[8,64,128,128]{3,2,1,0:T(8,128)(2,1)}, u32[]{:S(2)}, u32[]{:S(2)}) %all-to-all-start) | async-done | bytes 16777248 | tf_op jit(solution)/shard_map/all_to_all | solution.py:96
  471.5 14.1 copy.44
  485.6 904.2 %while.12 = (s32[]{:T(128)}, bf16[64,512,128]{2,1,0:T(8,128)(2,1)}, bf16[64,1024,128]{2,1,0:T(8,128)(2,1)}, s32[]{:T(128)}, bf16[128,128]{1,0:T(8,128)(2,1)S(1)}...) while((s32[]{:T(128)}, bf16[64,512,128]{2,1,0:T(8,128)(2,1)}, ...), condition=%wide.region_5.6_spmd, body=%wide.region_2.5_spmd.sunk | while | flops 535695360 | bytes 21415556 | solution.py:106
  492.4 6.2 fusion.83
  506.5 6.2 fusion.83
  520.6 6.2 fusion.83
  548.9 6.2 fusion.83
  563.0 6.2 fusion.83
  591.3 6.2 fusion.83
  605.4 6.2 fusion.83
  633.7 6.2 fusion.83
  647.8 6.2 fusion.83
  676.0 6.2 fusion.83
  690.2 6.2 fusion.83
  718.4 6.2 fusion.83
  732.6 6.2 fusion.83
  760.8 6.2 fusion.83
  774.9 6.2 fusion.83
  803.2 6.2 fusion.83
  817.3 6.2 fusion.83
  845.6 6.2 fusion.83
  859.7 6.2 fusion.83
  888.0 6.2 fusion.83
  902.1 6.2 fusion.83
  930.3 6.2 fusion.83
  944.5 6.2 fusion.83
  972.7 6.2 fusion.83
  986.9 6.2 fusion.83
  1015.1 6.2 fusion.83
  1029.2 6.2 fusion.83
  1057.5 6.2 fusion.83
  1071.6 6.2 fusion.83
  1099.9 6.2 fusion.83
  1114.0 6.2 fusion.83
  1142.3 6.2 fusion.83
  1156.4 6.2 fusion.83
  1184.6 6.2 fusion.83
  1354.2 6.2 fusion.83
  1389.8 9.5 copy.49
  1399.3 187.1 %all_to_all.49 = bf16[64,8,2,32,128]{4,3,2,0,1:T(8,128)(2,1)} all-to-all(bf16[64,8,2,32,128]{4,3,2,0,1:T(8,128)(2,1)} %copy.49), channel_id=1, replica_groups=mesh['row'=4,'col'=8] {'col'}, dimensions={1} | all-to-all | bytes 16777216 | tf_op jit(solution)/shard_map/all_to_all | solution.py:110
  1586.4 9.4 copy.50
  (579 shorter events, 698.5 us)
Async XLA Ops:
  6.5 27.0 %copy-start = (f32[128,4]{0,1:T(4,128)S(1)}, f32[128,4]{0,1:T(4,128)}, u32[]{:S(2)}) copy-start(f32[128,4]{0,1:T(4,128)} %param.21) | copy-start | bytes 6148
  6.5 16.9 %slice-start = ((s8[8388608]{0:T(1024)(128)(4,1)}), s8[4194304]{0:T(1024)(128)(4,1)S(1)}, s32[]{:S(2)}) async-start(s8[8388608]{0:T(1024)(128)(4,1)} %bitcast.105), calls=%async_computation.4 | async-start | bytes 8388608
  6.5 16.9 %copy-start.6 = (f32[128]{0:T(128)S(1)}, f32[128]{0:T(128)}, u32[]{:S(2)}) copy-start(f32[128]{0:T(128)} %param.14) | copy-start | bytes 1540
  6.5 16.9 %copy-start.5 = (f32[128]{0:T(128)S(1)}, f32[128]{0:T(128)}, u32[]{:S(2)}) copy-start(f32[128]{0:T(128)} %param.15) | copy-start | bytes 1540
  12.4 11.1 slice-start.1
  103.8 367.7 %all-to-all-start = ((bf16[8,64,128,128]{3,2,1,0:T(8,128)(2,1)}), bf16[8,64,128,128]{3,2,1,0:T(8,128)(2,1)}, u32[]{:S(2)}, u32[]{:S(2)}) async-start(bf16[8,64,128,128]{3,2,1,0:T(8,128)(2,1)} %bitcast.107), calls=%async_computation | async-start | bytes 33554432 | tf_op jit(solution)/shard_map/all_to_all | solution.py:96
  109.5 63.2 %all-gather.2.cloned.1.call-start = ((), (), s32[]{:S(2)}) async-start(), calls=%async_computation.3 | async-start | bytes 10485760 | tf_op jit(solution)/shard_map/all_gather | solution.py:88
  181.0 304.5 %copy-start.2 = (bf16[128,128]{1,0:T(8,128)(2,1)S(1)}, bf16[128,128]{1,0:T(8,128)(2,1)}, u32[]{:S(2)}) copy-start(bf16[128,128]{1,0:T(8,128)(2,1)} %param.18) | copy-start | bytes 98308
  181.0 304.5 %copy-start.3 = (bf16[128,128]{1,0:T(8,128)(2,1)S(1)}, bf16[128,128]{1,0:T(8,128)(2,1)}, u32[]{:S(2)}) copy-start(bf16[128,128]{1,0:T(8,128)(2,1)} %param.16) | copy-start | bytes 98308
  181.1 304.5 %copy-start.4 = (bf16[128,128]{1,0:T(8,128)(2,1)S(1)}, bf16[128,128]{1,0:T(8,128)(2,1)}, u32[]{:S(2)}) copy-start(bf16[128,128]{1,0:T(8,128)(2,1)} %param.17) | copy-start | bytes 98308
  181.1 304.5 %copy-start.7 = (bf16[128,128]{1,0:T(8,128)(2,1)S(1)}, bf16[128,128]{1,0:T(8,128)(2,1)}, u32[]{:S(2)}) copy-start(bf16[128,128]{1,0:T(8,128)(2,1)} %param.19) | copy-start | bytes 98308
  181.1 304.5 %copy-start.8 = (bf16[128,128]{1,0:T(8,128)(2,1)S(1)}, bf16[128,128]{1,0:T(8,128)(2,1)}, u32[]{:S(2)}) copy-start(bf16[128,128]{1,0:T(8,128)(2,1)} %param.22) | copy-start | bytes 98308
  181.1 304.5 %copy-start.9 = (f32[128]{0:T(128)S(1)}, f32[128]{0:T(128)}, u32[]{:S(2)}) copy-start(f32[128]{0:T(128)} %param.20) | copy-start | bytes 1540
  181.1 304.5 %copy-start.10 = (f32[128]{0:T(128)S(1)}, f32[128]{0:T(128)}, u32[]{:S(2)}) copy-start(f32[128]{0:T(128)} %param.23) | copy-start | bytes 1540
  1586.4 9.4 copy-start.1
Sparse Core Ops, SparseCore 0:
  113.4 59.3 all-gather.1
where the time goes:
time: 1610 us; the launch traced here: 1600 us
  matrix products  836 us (52%)
  waiting for transfers between devices  350 us (22%)
  blocking collectives  242 us (15%)
  local copies, waits for them, and re-layouts  125 us (8%)
  other arithmetic  26.9 us (2%)
    dot_general x64, matrix products, attend_one(): jnp.einsum('hjk,khd->jhd', weights, value, preferred_element_type=jnp.flo...  399 us
    sub x64, matrix products, attend_one(): raised = jnp.exp(scores - largest)  318 us
    all_to_all x1, waiting for transfers between devices, on_device(): lax.all_to_all(send_rows, 'col', split_axis=0, concat_axis=2, tiled=True)[0]  290 us
    all_to_all x1, blocking collectives, on_device(): lax.all_to_all(blocks, 'col', split_axis=1, concat_axis=0, tiled=True)  187 us
    dot_general x64, matrix products, attend_one(): jnp.dot(gated, w_out, preferred_element_type=jnp.float32) + out_shift  63.9 us
    dynamic_slice x64, local copies, waits for them, and re-layouts, on_device(): update_part = lax.map(row_update, my_rows)  61.9 us
    all_gather x1, waiting for transfers between devices, on_device(): group_bias = lax.all_gather(got_bias, 'row', axis=1, tiled=True)  59.5 us
    all_to_all x1, blocking collectives, on_device(): lax.all_to_all(send_bias, 'col', split_axis=1, concat_axis=4, tiled=True)  55.3 us
  transfers between devices with their start and end apart: 2, of which 2 were waited for; matrix products, arithmetic and copies ran while one was open for 1% of the time, Pallas kernels for 0%

commit v1 on v0

v1 whole, which is shorter than its diff:
```python
import functools
import math

import jax
import jax.numpy as jnp
from jax import lax
from jax.experimental import pallas as pl
from jax.experimental.pallas import tpu as pltpu
from jax.sharding import PartitionSpec as P

F32 = jnp.float32
BF16 = jnp.bfloat16
VMEM_LIMIT = 62 * 1024 * 1024


def nt_dot(a, b):
    return lax.dot_general(a, b, (((1,), (1,)), ((), ())), preferred_element_type=F32)


def norm_body(pair_ref, gain_ref, shift_ref, wbt_ref, normed_ref, bias_ref):
    rows, cols, channels = pair_ref.shape
    heads = bias_ref.shape[0]
    values = pair_ref[...].reshape(rows * cols, channels).astype(F32)
    mean = jnp.mean(values, axis=-1, keepdims=True)
    centred = values - mean
    spread = jnp.mean(centred * centred, axis=-1, keepdims=True)
    normed = (centred * lax.rsqrt(spread + 1e-05) * gain_ref[...] + shift_ref[...]).astype(BF16)
    normed_ref[...] = normed.reshape(rows, cols, channels)
    wbt = wbt_ref[...]
    high = wbt.astype(BF16)
    rest = wbt - high.astype(F32)
    mid = rest.astype(BF16)
    low = (rest - mid.astype(F32)).astype(BF16)
    bias = nt_dot(high, normed) + (nt_dot(mid, normed) + nt_dot(low, normed))
    for j in range(rows):
        bias_ref[:, j, :] = bias[:heads, j * cols : (j + 1) * cols]


def normalize(pair, gain, shift, w_bias):
    tile_rows, tile_cols, channels = pair.shape
    heads = w_bias.shape[1]
    pad = -heads % 16
    wbt = jnp.pad(w_bias.T, ((0, pad), (0, 0)))
    step = 16
    return pl.pallas_call(
        norm_body,
        grid=(tile_rows // step,),
        in_specs=[
            pl.BlockSpec((step, tile_cols, channels), lambda i: (i, 0, 0)),
            pl.BlockSpec((1, channels), lambda i: (0, 0)),
            pl.BlockSpec((1, channels), lambda i: (0, 0)),
            pl.BlockSpec(wbt.shape, lambda i: (0, 0)),
        ],
        out_specs=[
            pl.BlockSpec((step, tile_cols, channels), lambda i: (i, 0, 0)),
            pl.BlockSpec((heads, step, tile_cols), lambda i: (0, i, 0)),
        ],
        out_shape=[
            jax.ShapeDtypeStruct(pair.shape, BF16),
            jax.ShapeDtypeStruct((heads, tile_rows, tile_cols), F32),
        ],
        name="norm_bias",
    )(pair, gain[None], shift[None], wbt)


def project(x, wq_ref, wkt_ref, wv_ref, q_ref, kt_ref, v_ref, heads):
    inner = wq_ref.shape[1]
    depth = inner // heads
    query = (jnp.dot(x, wq_ref[...], preferred_element_type=F32) * (1.0 / math.sqrt(depth)))
    value = jnp.dot(x, wv_ref[...], preferred_element_type=F32)
    kt_ref[...] = nt_dot(wkt_ref[...], x).astype(BF16)
    head_of = lax.broadcasted_iota(jnp.int32, query.shape, 1) // depth
    for h in range(heads):
        q_ref[h] = jnp.where(head_of == h, query, 0.0).astype(BF16)
        v_ref[h] = jnp.where(head_of == h, value, 0.0).astype(BF16)


def attend_block(x, start, size, bias_of, q_ref, kt_ref, v_ref, wg, gshift, wo, oshift, heads):
    attended = None
    for h in range(heads):
        scores = jnp.dot(
            q_ref[h, pl.ds(start, size), :], kt_ref[...], preferred_element_type=F32
        ) + bias_of(h)
        largest = jnp.max(scores, axis=1, keepdims=True)
        raised = jnp.exp(scores - largest)
        scale = 1.0 / jnp.sum(raised, axis=1, keepdims=True)
        weights = (raised * scale).astype(BF16)
        part = jnp.dot(weights, v_ref[h], preferred_element_type=F32)
        attended = part if attended is None else attended + part
    gate = jax.nn.sigmoid(jnp.dot(x, wg, preferred_element_type=F32) + gshift)
    gated = (gate * attended).astype(BF16)
    return (jnp.dot(gated, wo, preferred_element_type=F32) + oshift).astype(BF16)


def attend_body(
    x_ref, bias_ref, wq_ref, wkt_ref, wv_ref, wg_ref, gshift_ref, wo_ref, oshift_ref,
    out_ref, q_ref, kt_ref, v_ref, x_flat, o_flat, *, block,
):
    pieces, heads = bias_ref.shape[0], bias_ref.shape[1]
    length, channels = x_flat.shape
    x_flat[...] = x_ref[...].reshape(length, channels)
    project(x_flat[...], wq_ref, wkt_ref, wv_ref, q_ref, kt_ref, v_ref, heads)

    @pl.loop(0, length // block)
    def _(b):
        start = pl.multiple_of(b * block, block)

        def bias_of(h):
            parts = [bias_ref[p, h, pl.ds(start, block), :] for p in range(pieces)]
            return parts[0] if pieces == 1 else jnp.concatenate(parts, axis=1)

        o_flat[pl.ds(start, block), :] = attend_block(
            x_flat[pl.ds(start, block), :], start, block, bias_of, q_ref, kt_ref, v_ref,
            wg_ref[...], gshift_ref[...], wo_ref[...], oshift_ref[...], heads,
        )

    out_ref[...] = o_flat[...].reshape(out_ref.shape)


def attend(rows, bias, w_query, w_key, w_value, w_gate, gate_shift, w_out, out_shift, block=512):
    groups, count, cols, channels = rows.shape
    length = groups * cols
    heads = bias.shape[1]
    inner = w_query.shape[1]
    whole = lambda a: pl.BlockSpec(a.shape, lambda i: (0,) * a.ndim, pipeline_mode=pl.Buffered(1))
    args = (bias, w_query, w_key.T, w_value, w_gate, gate_shift[None], w_out, out_shift[None])
    row_spec = pl.BlockSpec((groups, 1, cols, channels), lambda i: (0, i, 0, 0))
    return pl.pallas_call(
        functools.partial(attend_body, block=block),
        grid=(count,),
        in_specs=[row_spec] + [whole(a) for a in args],
        out_specs=row_spec,
        out_shape=jax.ShapeDtypeStruct(rows.shape, BF16),
        scratch_shapes=[
            pltpu.VMEM((heads, length, inner), BF16),
            pltpu.VMEM((inner, length), BF16),
            pltpu.VMEM((heads, length, inner), BF16),
            pltpu.VMEM((length, channels), BF16),
            pltpu.VMEM((length, channels), BF16),
        ],
        compiler_params=pltpu.CompilerParams(vmem_limit_bytes=VMEM_LIMIT),
        name="attend",
    )(rows, *args)


def on_device(
    pair, norm_gain, norm_shift, w_query, w_key, w_value, w_gate, gate_shift, w_bias, w_out,
    out_shift,
):
    col_count = lax.axis_size("col")
    row_count = lax.axis_size("row")
    tile_rows, tile_cols, channels = pair.shape
    heads = w_bias.shape[1]
    normed, tile_bias = normalize(pair, norm_gain, norm_shift, w_bias)
    by_row = lax.all_gather(tile_bias, "row", axis=1, tiled=True)
    bias = lax.all_gather(by_row, "col", axis=0)
    if tile_cols % 128:
        bias = bias.transpose(1, 2, 0, 3).reshape(1, heads, tile_rows * row_count, -1)
    blocks = normed.reshape(col_count, tile_rows // col_count, tile_cols, channels)
    rows = lax.all_to_all(blocks, "col", split_axis=0, concat_axis=0, tiled=True)
    update = attend(rows, bias, w_query, w_key, w_value, w_gate, gate_shift, w_out, out_shift)
    back = lax.all_to_all(update, "col", split_axis=0, concat_axis=0, tiled=True)
    return back.reshape(tile_rows, tile_cols, channels)


def solution(mesh):
    in_specs = (P("row", "col", None),) + (P(),) * 10
    return jax.shard_map(
        on_device, mesh=mesh, in_specs=in_specs, out_specs=P("row", "col", None), check_vma=False
    )
```

time: 1610 us -> 977 us (0.61)
  matrix products: 836 us -> 0 us
  Pallas kernels: 0 us -> 345 us
  local copies, waits for them, and re-layouts: 125 us -> 12.5 us
  waiting for transfers between devices: 350 us -> 411 us
  blocking collectives: 242 us -> 189 us
  other arithmetic: 26.9 us -> 0 us
    dot_general x321 -> x0, matrix products: 518 us -> none  [the longest x64 399 us: attend_one(): jnp.einsum('hjk,khd->jhd', weights, value, preferred_element_type=jnp.flo...]
    pallas_call x0 -> x2, Pallas kernels: none -> 345 us  [the longest x1 326 us: attend(): pl.pallas_call(functools.partial(attend_body, block=block), grid=(count,)...]
    sub x64 -> x0, matrix products: 318 us -> none  [attend_one(): raised = jnp.exp(scores - largest)]
    all_to_all x1, waiting for transfers between devices: 290 us -> 363 us  [on_device(): lax.all_to_all(blocks, 'col', split_axis=0, concat_axis=0, tiled=True)]
    dynamic_slice x128 -> x0, local copies, waits for them, and re-layouts: 63 us -> none  [the longest x64 61.9 us: on_device(): update_part = lax.map(row_update, my_rows)]
    all_to_all x2 -> x1, blocking collectives: 242 us -> 189 us  [on_device(): lax.all_to_all(update, 'col', split_axis=0, concat_axis=0, tiled=True)]
    reshape x65 -> x0, local copies, waits for them, and re-layouts: 17.9 us -> none  [the longest x1 9.51 us: on_device(): update_part.reshape(tile_rows // across, col_count, row_count // groups,...]
    all_to_all x3 -> x0, local copies, waits for them, and re-layouts: 17.5 us -> none  [the longest x1 14.1 us: on_device(): lax.all_to_all(send_rows, 'col', split_axis=0, concat_axis=2, tiled=True)[0]]
  transfers between devices with their start and end apart: 2 -> 3, of which waited for: 2 -> 3; matrix products, arithmetic and copies ran while one was open for 1% -> 0% of each run, Pallas kernels for 0% -> 0%
where the time goes in v1:
time: 977 us
  waiting for transfers between devices  411 us (42%)
  Pallas kernels  345 us (35%)
  blocking collectives  189 us (19%)
  between operations  13.4 us (1%)
  local copies, waits for them, and re-layouts  12.5 us (1%)
    all_to_all x1, waiting for transfers between devices, on_device(): lax.all_to_all(blocks, 'col', split_axis=0, concat_axis=0, tiled=True)  363 us
    pallas_call x1, Pallas kernels, attend(): pl.pallas_call(functools.partial(attend_body, block=block), grid=(count,)...  326 us
    all_to_all x1, blocking collectives, on_device(): lax.all_to_all(update, 'col', split_axis=0, concat_axis=0, tiled=True)  189 us
    all_gather x1, waiting for transfers between devices, on_device(): by_row = lax.all_gather(tile_bias, 'row', axis=1, tiled=True)  25.4 us
    all_gather x1, waiting for transfers between devices, on_device(): bias = lax.all_gather(by_row, 'col', axis=0)  22.8 us
  transfers between devices with their start and end apart: 3, of which 3 were waited for; matrix products, arithmetic and copies ran while one was open for 0% of the time, Pallas kernels for 0%

profile of v1, /device:TPU:0, one launch (start us, length us, event | category | flops | bytes accessed | tf_op | source)
XLA Modules:
  0.0 976.5 jit_solution(3065229553378948895)
XLA Ops:
  6.5 0.0 all-gather.4.cloned.1.call-start
  6.5 1.3 pad.4.wbt_ref
  7.8 18.3 %norm_bias.1 = (bf16[256,128,128]{2,1,0:T(8,128)(2,1)}, f32[4,256,128]{2,1,0:T(8,128)}) custom-call(bf16[256,128,128]{2,1,0:T(8,128)(2,1)} %pair_ref.1, f32[1,128]{1,0:T(1,128)} %bitcast.14, f32[1,128]{1,0:T(1,128)} %bitcast.15, f32[16,128]{1,0:T(8,128)} %pad.4.wbt_ref), custom_call_target="tpu_custom_call" | custom-call | tf_op jit(solution)/shard_map/norm_bias/pallas_call | solution.py:45
  26.1 0.0 all-gather.4.cloned.1.call-update
  26.1 0.0 all-gather.6.cloned.1.call-start
  26.2 25.4 %all-gather.4.cloned.1.call-done = f32[4,1024,128]{2,1,0:T(8,128)} async-done(((f32[4,256,128]{2,1,0:T(8,128)}), f32[4,1024,128]{2,1,0:T(8,128)}) %all-gather.4.cloned.1.call-update) | async-done | bytes 2097168 | tf_op jit(solution)/shard_map/all_gather | solution.py:155
  51.6 0.0 all-gather.6.cloned.1.call-update
  51.6 0.0 copy-start
  51.6 5.5 all-to-all-start
  57.1 0.0 copy-done
  57.1 0.7 copy.13
  57.9 362.9 %all-to-all-done.x_ref = bf16[8,32,128,128]{3,2,1,0:T(8,128)(2,1)} async-done(((bf16[8,32,128,128]{3,2,1,0:T(8,128)(2,1)}), bf16[8,32,128,128]{3,2,1,0:T(8,128)(2,1)}, u32[]{:S(2)}, u32[]{:S(2)}) %all-to-all-start) | async-done | bytes 8388640 | tf_op jit(solution)/shard_map/all_to_all | solution.py:160
  420.8 22.8 %all-gather.6.cloned.1.call-done = f32[32,1024,128]{2,1,0:T(8,128)} async-done(((f32[4,1024,128]{2,1,0:T(8,128)}), f32[32,1024,128]{2,1,0:T(8,128)}) %all-gather.6.cloned.1.call-update) | async-done | bytes 16777232 | tf_op jit(solution)/shard_map/all_gather | solution.py:156
  443.6 326.4 %attend.1 = bf16[8,32,128,128]{3,2,1,0:T(8,128)(2,1)} custom-call(bf16[8,32,128,128]{3,2,1,0:T(8,128)(2,1)} %all-to-all-done.x_ref, f32[8,4,1024,128]{3,2,1,0:T(8,128)} %bitcast.10, bf16[128,128]{1,0:T(8,128)(2,1)} %wq_ref.1, bf16[128,128]{1,0:T(8,128)(2,1)} %bitcast.12, bf16[128,128]{1,0:T(8,128)(2,1)} %wv_ref.1, bf16[128,128]{1,0:T(8,128)(2,1)} %wg_ref.1, ...), custom_call_target="tpu_custom_call" | custom-call | tf_op jit(solution)/shard_map/attend/pallas_call | solution.py:128
  770.0 189.2 %all_to_all.10 = bf16[8,32,128,128]{3,2,1,0:T(8,128)(2,1)} all-to-all(bf16[8,32,128,128]{3,2,1,0:T(8,128)(2,1)} %attend.1), channel_id=1, replica_groups=mesh['row'=4,'col'=8] {'col'}, dimensions={0} | all-to-all | bytes 16777216 | tf_op jit(solution)/shard_map/all_to_all | solution.py:162
  959.2 10.5 %copy.15 = bf16[256,128,128]{2,1,0:T(8,128)(2,1)} copy(bf16[256,128,128]{2,1,0:T(8,128)(2,1)} %bitcast.9) | data formatting | bytes 16777216
Async XLA Ops:
  6.5 45.0 %all-gather.4.cloned.1.call-start = ((), (), s32[]{:S(2)}) async-start(), calls=%async_computation.2 | async-start | bytes 2621440 | tf_op jit(solution)/shard_map/all_gather | solution.py:155
  26.1 417.4 %all-gather.6.cloned.1.call-start = ((), (), s32[]{:S(2)}) async-start(), calls=%async_computation.3 | async-start | bytes 18874368 | tf_op jit(solution)/shard_map/all_gather | solution.py:156
  51.6 5.5 copy-start
  51.6 369.2 %all-to-all-start = ((bf16[8,32,128,128]{3,2,1,0:T(8,128)(2,1)}), bf16[8,32,128,128]{3,2,1,0:T(8,128)(2,1)}, u32[]{:S(2)}, u32[]{:S(2)}) async-start(bf16[8,32,128,128]{3,2,1,0:T(8,128)(2,1)} %bitcast.11), calls=%async_computation | async-start | bytes 16777216 | tf_op jit(solution)/shard_map/all_to_all | solution.py:160
Sparse Core Ops, SparseCore 0:
  26.3 25.2 all-gather.3
  53.7 389.8 all-gather.5
